TPU v7x, 32 devices: a whole 2x2x4 slice. The times are simulated.
32 devices in a mesh: row: 16 (over z, x, core), col: 2 (over y).
Axes of the slice: x: 2, y: 2, z: 4, core: 2. Of those that a mesh axis runs over, the one named last changes fastest.
Arguments:
- row_features: bfloat16 [256, 256], P(('row', 'col')), may hold values from -6 to 6
- col_features: bfloat16 [512, 256], P(('col', 'row')), may hold values from -6 to 6
- row_proj: bfloat16 [256, 64], replicated, may hold values from -0.375 to 0.375
- col_proj: bfloat16 [256, 64], replicated, may hold values from -0.375 to 0.375
- pair_weight: bfloat16 [2, 3, 3, 64, 64], replicated, may hold values from -0.1875 to 0.1875
- pair_bias: float32 [64], replicated, may hold values from -4 to 4
- conv_weight: bfloat16 [3, 3, 64, 64], replicated, may hold values from -0.25 to 0.25
- dilations: int32 [2], replicated, may hold values from 1 to 8, as said below
- cotangent: bfloat16 [64, 256, 512], P(None, 'row', 'col'), may hold values from -6 to 6
Outputs:
- pair_out: bfloat16 [64, 256, 512], P(None, 'row', 'col')
- grad_row_features: float32 [256, 256], P(('row', 'col'))
- grad_col_features: float32 [512, 256], P(('col', 'row'))
- grad_row_proj: float32 [256, 64], replicated
- grad_col_proj: float32 [256, 64], replicated
- grad_pair_weight: float32 [2, 3, 3, 64, 64], replicated
- grad_pair_bias: float32 [64], replicated
- grad_conv_weight: float32 [3, 3, 64, 64], replicated
Inputs may be any that keep to these rules, and one draw needn't show every extreme that they name: One of the two dilations equals 8.
All inputs are finite; a program needn't handle non-finite values.
Results may differ from a plain program's by a relative error of at most 0.0054.
Values may be sent and summed in bfloat16 or wider, within the bound.
No kernel may reach another device: no remote copies, remote signals or barrier semaphores. Data moves between devices by JAX's collectives and lax.ppermute only.
A program may use at most 64 MiB of HBM per device.

v0:
```python
import jax
import jax.numpy as jnp
from jax import lax
from jax.sharding import PartitionSpec as P

MAX_DILATION = 8


def padded_2(value, sides, width):
    for axis, dim in sides:
        devices, length = (lax.axis_size(axis), value.shape[dim])
        up = [(i, (i + 1) % devices) for i in range(devices - 1)]
        down = [(j, i) for i, j in up]
        last = lax.slice_in_dim(value, length - width, length, axis=dim)
        leading = lax.slice_in_dim(value, 0, width, axis=dim)
        before = lax.ppermute(last, axis, up)
        after = lax.ppermute(leading, axis, down)
        value = jnp.concatenate([before, value, after], axis=dim)
    return value


def project(features, weight):
    return jnp.dot(features, weight, preferred_element_type=jnp.float32).astype(jnp.bfloat16)


def line_terms(padded, weights, dilation, count, offset):
    shifted = jnp.stack(
        [
            lax.dynamic_slice_in_dim(padded, offset + (tap_idx - 1) * dilation, count, 0)
            for tap_idx in range(3)
        ]
    )
    return jnp.einsum("kip,kqpo->qio", shifted, weights, preferred_element_type=jnp.float32)


def line_valid(first_cell, count, cell_limit, dilation):
    cells = first_cell + jnp.arange(count, dtype=jnp.int32)
    columns = [
        (cells + (tap_idx - 1) * dilation >= 0) & (cells + (tap_idx - 1) * dilation < cell_limit)
        for tap_idx in range(3)
    ]
    return jnp.stack(columns, axis=1).astype(jnp.float32)


def pair_field(row_terms, col_terms, row_valid, col_valid, bias):
    from_rows = jnp.einsum("jq,qic->cij", col_valid, row_terms, precision=lax.Precision.HIGHEST)
    from_cols = jnp.einsum("ik,kjc->cij", row_valid, col_terms, precision=lax.Precision.HIGHEST)
    return from_rows + from_cols + bias[:, None, None]


def window_at(padded, row_index, col_index, rows, cols):
    anchor = jnp.zeros((), jnp.int32)
    return lax.dynamic_slice(padded, (anchor, row_index, col_index), (padded.shape[0], rows, cols))


def conv_taps(padded, weight, dilation, rows, cols, margin):
    result = jnp.zeros((weight.shape[3], rows, cols), jnp.float32)
    for tap_row in range(3):
        for tap_col in range(3):
            window = window_at(
                padded,
                margin + (tap_row - 1) * dilation,
                margin + (tap_col - 1) * dilation,
                rows,
                cols,
            )
            result = result + jnp.einsum(
                "co,cij->oij", weight[tap_row, tap_col], window, preferred_element_type=jnp.float32
            )
    return result


def back_taps(padded, weight, dilation, rows, cols, margin):
    result = jnp.zeros((weight.shape[2], rows, cols), jnp.float32)
    for tap_row in range(3):
        for tap_col in range(3):
            window = window_at(
                padded,
                margin - (tap_row - 1) * dilation,
                margin - (tap_col - 1) * dilation,
                rows,
                cols,
            )
            result = result + jnp.einsum(
                "co,oij->cij", weight[tap_row, tap_col], window, preferred_element_type=jnp.float32
            )
    return result


def tap_grads(hidden_pad, grads, dilation, rows, cols, margin):
    stacked = []
    for tap_row in range(3):
        line_list = []
        for tap_col in range(3):
            window = window_at(
                hidden_pad,
                margin + (tap_row - 1) * dilation,
                margin + (tap_col - 1) * dilation,
                rows,
                cols,
            )
            line_list.append(
                jnp.einsum("cij,oij->co", window, grads, preferred_element_type=jnp.float32)
            )
        stacked.append(jnp.stack(line_list))
    return jnp.stack(stacked)


def shards(
    row_features,
    col_features,
    row_proj,
    col_proj,
    pair_weight,
    pair_bias,
    conv_weight,
    dilations,
    cotangent,
):
    first_rate = dilations[0]
    second_rate = dilations[1]
    margin = MAX_DILATION
    row_count = lax.axis_size("row")
    col_count = lax.axis_size("col")
    row_place = lax.axis_index("row")
    col_place = lax.axis_index("col")
    rows_here = cotangent.shape[1]
    cols_here = cotangent.shape[2]
    row_start = row_place * rows_here
    col_start = col_place * cols_here
    row_limit = rows_here * row_count
    col_limit = cols_here * col_count
    row_piece = row_features.shape[0]
    col_piece = col_features.shape[0]
    rows_a = lax.all_gather(project(row_features, row_proj), "col", axis=0, tiled=True)
    cols_b = lax.all_gather(project(col_features, col_proj), "row", axis=0, tiled=True)
    pad_extra = 0
    a_pad = padded_2(rows_a, (("row", 0),), MAX_DILATION)
    b_pad = padded_2(cols_b, (("col", 0),), MAX_DILATION)
    row_terms = line_terms(
        a_pad, pair_weight[0], first_rate, rows_here + 2 * pad_extra, margin - pad_extra
    )
    col_terms = line_terms(
        b_pad,
        jnp.swapaxes(pair_weight[1], 0, 1),
        first_rate,
        cols_here + 2 * pad_extra,
        margin - pad_extra,
    )
    row_valid = line_valid(row_start - pad_extra, rows_here + 2 * pad_extra, row_limit, first_rate)
    col_valid = line_valid(col_start - pad_extra, cols_here + 2 * pad_extra, col_limit, first_rate)
    pre_act = pair_field(row_terms, col_terms, row_valid, col_valid, pair_bias)
    hidden_own = jax.nn.silu(pre_act).astype(jnp.bfloat16)
    hidden = padded_2(hidden_own, (("row", 1), ("col", 2)), MAX_DILATION)
    conv_mixed = conv_taps(hidden, conv_weight, second_rate, rows_here, cols_here, margin)
    pair_out = (hidden_own.astype(jnp.float32) + conv_mixed).astype(jnp.bfloat16)
    grad_pad = padded_2(cotangent, (("row", 1), ("col", 2)), MAX_DILATION)
    d_hidden = cotangent.astype(jnp.float32) + back_taps(
        grad_pad, conv_weight, second_rate, rows_here, cols_here, margin
    )
    conv_grad = tap_grads(hidden, cotangent, second_rate, rows_here, cols_here, margin)
    sigmoid_own = jax.nn.sigmoid(pre_act)
    d_pre = d_hidden * sigmoid_own * (1.0 + pre_act * (1.0 - sigmoid_own))
    bias_grad = jnp.sum(d_pre, axis=(1, 2))
    row_valid_own = line_valid(row_start, rows_here, row_limit, first_rate)
    col_valid_own = line_valid(col_start, cols_here, col_limit, first_rate)
    row_part = jnp.einsum("jq,cij->qic", col_valid_own, d_pre, precision=lax.Precision.HIGHEST)
    col_part = jnp.einsum("ik,cij->kjc", row_valid_own, d_pre, precision=lax.Precision.HIGHEST)
    row_sums = lax.psum(row_part, "col")
    col_sums = lax.psum(col_part, "row")
    back_rows = jnp.einsum(
        "qio,kqpo->kip",
        row_sums,
        pair_weight[0].astype(jnp.float32),
        precision=lax.Precision.HIGHEST,
    )
    back_cols = jnp.einsum(
        "kjo,kqpo->qjp",
        col_sums,
        pair_weight[1].astype(jnp.float32),
        precision=lax.Precision.HIGHEST,
    )
    rows_back_pad = padded_2(back_rows, (("row", 1),), MAX_DILATION)
    cols_back_pad = padded_2(back_cols, (("col", 1),), MAX_DILATION)
    row_own = col_place * row_piece
    col_own = row_place * col_piece
    d_rows = sum(
        (
            lax.dynamic_slice_in_dim(
                rows_back_pad[tap_idx], margin + row_own - (tap_idx - 1) * first_rate, row_piece, 0
            )
            for tap_idx in range(3)
        )
    )
    d_cols = sum(
        (
            lax.dynamic_slice_in_dim(
                cols_back_pad[tap_idx], margin + col_own - (tap_idx - 1) * first_rate, col_piece, 0
            )
            for tap_idx in range(3)
        )
    )
    d_rows = d_rows.astype(jnp.bfloat16)
    d_cols = d_cols.astype(jnp.bfloat16)
    grad_row_features = jnp.dot(d_rows, row_proj.T, preferred_element_type=jnp.float32)
    grad_col_features = jnp.dot(d_cols, col_proj.T, preferred_element_type=jnp.float32)
    grad_row_proj = jnp.dot(row_features.T, d_rows, preferred_element_type=jnp.float32)
    grad_col_proj = jnp.dot(col_features.T, d_cols, preferred_element_type=jnp.float32)
    row_shifted = jnp.stack(
        [
            lax.dynamic_slice_in_dim(
                a_pad, margin + row_own + (tap_idx - 1) * first_rate, row_piece, 0
            )
            for tap_idx in range(3)
        ]
    )
    col_shifted = jnp.stack(
        [
            lax.dynamic_slice_in_dim(
                b_pad, margin + col_own + (tap_idx - 1) * first_rate, col_piece, 0
            )
            for tap_idx in range(3)
        ]
    )
    row_sums_own = lax.dynamic_slice_in_dim(row_sums, row_own, row_piece, 1)
    col_sums_own = lax.dynamic_slice_in_dim(col_sums, col_own, col_piece, 1)
    grad_row_pair = jnp.einsum(
        "kip,qio->kqpo",
        row_shifted.astype(jnp.float32),
        row_sums_own,
        precision=lax.Precision.HIGHEST,
    )
    grad_col_pair = jnp.einsum(
        "qjp,kjo->kqpo",
        col_shifted.astype(jnp.float32),
        col_sums_own,
        precision=lax.Precision.HIGHEST,
    )
    summed = lax.psum(
        (
            grad_row_proj,
            grad_col_proj,
            jnp.stack([grad_row_pair, grad_col_pair]),
            bias_grad,
            conv_grad,
        ),
        ("row", "col"),
    )
    return (
        pair_out,
        grad_row_features,
        grad_col_features,
        summed[0],
        summed[1],
        summed[2],
        summed[3],
        summed[4],
    )


def solution(mesh):
    return jax.shard_map(
        shards,
        mesh=mesh,
        in_specs=(
            P(("row", "col"), None),
            P(("col", "row"), None),
            P(),
            P(),
            P(),
            P(),
            P(),
            P(),
            P(None, "row", "col"),
        ),
        out_specs=(
            P(None, "row", "col"),
            P(("row", "col"), None),
            P(("col", "row"), None),
            P(),
            P(),
            P(),
            P(),
            P(),
        ),
        check_vma=False,
    )
```

profile of v0, /device:TPU:0, one launch (start us, length us, event | category | flops | bytes accessed | tf_op | source)
XLA Modules:
  0.0 352.3 jit_solution(3747171923452874970)
XLA Ops:
  8.7 23.3 %all_gather.7 = bf16[256,64]{1,0:T(8,128)(2,1)S(1)} all-gather(bf16[16,64]{1,0:T(8,128)(2,1)S(1)} %convolution_convert_fusion), channel_id=1, replica_groups=mesh['row'=16,'col'=2] {'row'}, dimensions={0}, use_global_device_ids=true | all-gather | bytes 34816 | tf_op jit(solution)/shard_map/all_gather | solution.py:136
  32.0 3.4 collective-permute-start.2
  37.6 5.0 %all_gather.6 = bf16[16,64]{1,0:T(8,128)(2,1)S(1)} all-gather(bf16[8,64]{1,0:T(8,128)(2,1)S(1)} %convolution_convert_fusion.1), channel_id=1, replica_groups=mesh['row'=16,'col'=2] {'col'}, dimensions={0}, use_global_device_ids=true | all-gather | bytes 3072 | tf_op jit(solution)/shard_map/all_gather | solution.py:135
  47.0 3.7 %collective-permute-start.8 = (bf16[64,8,256]{2,0,1:T(8,128)(2,1)}, bf16[64,8,256]{2,0,1:T(8,128)(2,1)}, u32[]{:S(2)}, u32[]{:S(2)}) collective-permute-start(bf16[64,8,256]{2,0,1:T(8,128)(2,1)} %copy.143), channel_id=1, source_target_pairs={{0,2},{2,4},{4,6},{6,8},{8,10},{10,12},{12,14},{14,16},{16,18},{18... | collective-permute-start | bytes 786440 | tf_op jit(solution)/shard_map/ppermute | solution.py:16
  67.0 1.4 multiply_convert_fusion
  68.8 3.0 collective-permute-start.4
  75.0 4.0 %collective-permute-start.10 = (bf16[64,32,8]{2,0,1:T(8,128)(2,1)S(1)}, bf16[64,32,8]{2,0,1:T(8,128)(2,1)S(1)}, u32[]{:S(2)}, u32[]{:S(2)}) collective-permute-start(bf16[64,32,8]{2,0,1:T(8,128)(2,1)S(1)} %get-tuple-element.20), channel_id=1, source_target_pairs={{0,1},{2,3},{4,5},{6,7},{8,9},{10,11},{12,13},{14,15},{16,17},{18,... | collective-permute-start | bytes 98312 | tf_op jit(solution)/shard_map/ppermute | solution.py:16
  81.7 5.4 %collective-permute-start.6 = (bf16[64,32,8]{2,0,1:T(8,128)(2,1)}, bf16[64,32,8]{2,0,1:T(8,128)(2,1)}, u32[]{:S(2)}, u32[]{:S(2)}) collective-permute-start(bf16[64,32,8]{2,0,1:T(8,128)(2,1)} %get-tuple-element.22), channel_id=1, source_target_pairs={{0,1},{2,3},{4,5},{6,7},{8,9},{10,11},{12,13},{14,15},{16,17},{18,... | collective-permute-start | bytes 98312 | tf_op jit(solution)/shard_map/ppermute | solution.py:16
  87.1 1.5 collective-permute-start.7
  88.6 2.0 collective-permute-done.10
  90.5 4.7 %collective-permute-done.11 = bf16[64,32,8]{2,0,1:T(8,128)(2,1)S(1)} collective-permute-done((bf16[64,32,8]{2,0,1:T(8,128)(2,1)S(1)}, bf16[64,32,8]{2,0,1:T(8,128)(2,1)S(1)}, u32[]{:S(2)}, u32[]{:S(2)}) %collective-permute-start.11) | collective-permute-done | bytes 32800 | tf_op jit(solution)/shard_map/ppermute | solution.py:17
  100.2 1.8 convolution_bitcast_fusion.7
  103.0 8.6 %psum.49 = f32[3,16,64]{1,0,2:T(4,128)S(1)} all-reduce(f32[3,16,64]{1,0,2:T(4,128)S(1)} %bitcast.308), channel_id=1, replica_groups=mesh['row'=16,'col'=2] {'col'}, use_global_device_ids=true, to_apply=%region_0.1 | all-reduce | flops 3072 | bytes 24576 | tf_op jit(solution)/shard_map/psum | solution.py:169
  113.1 1.5 collective-permute-start.12
  114.6 1.3 collective-permute-start.13
  116.2 47.7 %psum.54 = f32[64]{0:T(128)} all-reduce(f32[64]{0:T(128)S(1)} %get-tuple-element.56), channel_id=1, replica_groups=mesh['row'=16,'col'=2] {'row','col'}, use_global_device_ids=true, to_apply=%region_6.7 | all-reduce | flops 64 | bytes 512 | tf_op jit(solution)/shard_map/psum | solution.py:239
  163.9 2.2 pad_maximum_fusion
  176.3 19.0 %all-reduce.4.cloned.1.call-done = f32[3,256,64]{1,0,2:T(4,128)} async-done(((f32[3,256,64]{1,0,2:T(4,128)}), f32[3,256,64]{1,0,2:T(4,128)}) %all-reduce.4.cloned.1.call-update) | async-done | bytes 196624 | tf_op jit(solution)/shard_map/psum | solution.py:170
  197.8 3.5 collective-permute-start.14
  203.8 4.1 %collective-permute-done.15 = f32[3,8,64]{1,2,0:T(8,128)S(1)} collective-permute-done((f32[3,8,64]{1,2,0:T(8,128)S(1)}, f32[3,8,64]{1,2,0:T(8,128)S(1)}, u32[]{:S(2)}, u32[]{:S(2)}) %collective-permute-start.15) | collective-permute-done | bytes 6176 | tf_op jit(solution)/shard_map/ppermute | solution.py:17
  210.5 129.1 %all-reduce.6.cloned.1.call-done = (f32[256,64]{0,1:T(8,128)}, f32[256,64]{0,1:T(8,128)}, f32[2,3,3,64,64]{3,4,1,2,0:T(8,128)}, f32[3,3,64,64]{3,2,1,0:T(8,128)}) async-done(((f32[256,64]{0,1:T(8,128)}, f32[256,64]{0,1:T(8,128)}, f32[2,3,3,64,64]{3,4,1,2,0:T(8,128)}, f32[3,3,64,64]{3,2,1,0:T(8,128)}), (f32[256,64]{0,1:T(8,128)}, f32[256,64]{0,1:T(8,128)}, f32[2,3,3,64,64]{3,4,1,2,0:T(8,128)}, ...) | async-done | bytes 573456 | tf_op jit(solution)/shard_map/psum | solution.py:239
  339.6 2.1 copy.59
  341.8 1.5 copy.158
  343.2 1.5 copy.159
  (141 shorter events, 46.2 us)
Async XLA Ops:
  7.2 56.0 %copy-start.1 = (bf16[64,16,256]{2,1,0:T(8,128)(2,1)S(1)}, bf16[64,16,256]{2,1,0:T(8,128)(2,1)}, u32[]{:S(2)}) copy-start(bf16[64,16,256]{2,1,0:T(8,128)(2,1)} %param.17) | copy-start | bytes 1572868
  7.2 43.5 %copy-start.12 = (s32[2]{0:T(128)S(1)}, s32[2]{0:T(128)}, u32[]{:S(2)}) copy-start(s32[2]{0:T(128)} %param.16) | copy-start | bytes 28
  7.2 188.1 %all-reduce.4.cloned.1.call-start = ((), (), s32[]{:S(2)}) async-start(), calls=%async_computation | async-start | bytes 524288 | tf_op jit(solution)/shard_map/psum | solution.py:170
  32.0 32.3 %collective-permute-start.2 = (bf16[8,64]{1,0:T(8,128)(2,1)S(1)}, bf16[8,64]{1,0:T(8,128)(2,1)S(1)}, u32[]{:S(2)}, u32[]{:S(2)}) collective-permute-start(bf16[8,64]{1,0:T(8,128)(2,1)S(1)} %get-tuple-element.39), channel_id=1, source_target_pairs={{0,1},{2,3},{4,5},{6,7},{8,9},{10,11},{12,13},{14,15},{16,17},{18,... | collective-permute-start | bytes 3080 | tf_op jit(solution)/shard_map/ppermute | solution.py:16
  35.4 30.3 %collective-permute-start.3 = (bf16[8,64]{1,0:T(8,128)(2,1)S(1)}, bf16[8,64]{1,0:T(8,128)(2,1)S(1)}, u32[]{:S(2)}, u32[]{:S(2)}) collective-permute-start(bf16[8,64]{1,0:T(8,128)(2,1)S(1)} %get-tuple-element.38), channel_id=1, source_target_pairs={{1,0},{3,2},{5,4},{7,6},{9,8},{11,10},{13,12},{15,14},{17,16},{19,... | collective-permute-start | bytes 3080 | tf_op jit(solution)/shard_map/ppermute | solution.py:17
  42.6 23.2 %collective-permute-start = (bf16[8,64]{1,0:T(8,128)(2,1)S(1)}, bf16[8,64]{1,0:T(8,128)(2,1)S(1)}, u32[]{:S(2)}, u32[]{:S(2)}) collective-permute-start(bf16[8,64]{1,0:T(8,128)(2,1)S(1)} %get-tuple-element.51), channel_id=1, source_target_pairs={{0,2},{2,4},{4,6},{6,8},{8,10},{10,12},{12,14},{14,16},{16,18},{18... | collective-permute-start | bytes 3080 | tf_op jit(solution)/shard_map/ppermute | solution.py:16
  43.9 21.9 %collective-permute-start.1 = (bf16[8,64]{1,0:T(8,128)(2,1)S(1)}, bf16[8,64]{1,0:T(8,128)(2,1)S(1)}, u32[]{:S(2)}, u32[]{:S(2)}) collective-permute-start(bf16[8,64]{1,0:T(8,128)(2,1)S(1)} %get-tuple-element.50), channel_id=1, source_target_pairs={{2,0},{4,2},{6,4},{8,6},{10,8},{12,10},{14,12},{16,14},{18,16},{20... | collective-permute-start | bytes 3080 | tf_op jit(solution)/shard_map/ppermute | solution.py:17
  46.2 19.6 %copy-start.7 = (bf16[2,3,3,64,64]{4,3,2,1,0:T(8,128)(2,1)S(1)}, bf16[2,3,3,64,64]{4,3,2,1,0:T(8,128)(2,1)}, u32[]{:S(2)}) copy-start(bf16[2,3,3,64,64]{4,3,2,1,0:T(8,128)(2,1)} %param.13) | copy-start | bytes 442372
  47.0 26.5 %collective-permute-start.8 = (bf16[64,8,256]{2,0,1:T(8,128)(2,1)}, bf16[64,8,256]{2,0,1:T(8,128)(2,1)}, u32[]{:S(2)}, u32[]{:S(2)}) collective-permute-start(bf16[64,8,256]{2,0,1:T(8,128)(2,1)} %copy.143), channel_id=1, source_target_pairs={{0,2},{2,4},{4,6},{6,8},{8,10},{10,12},{12,14},{14,16},{16,18},{18... | collective-permute-start | bytes 786440 | tf_op jit(solution)/shard_map/ppermute | solution.py:16
  64.3 10.3 %collective-permute-start.9 = (bf16[64,8,256]{2,0,1:T(8,128)(2,1)}, bf16[64,8,256]{2,0,1:T(8,128)(2,1)S(1)}, u32[]{:S(2)}, u32[]{:S(2)}) collective-permute-start(bf16[64,8,256]{2,0,1:T(8,128)(2,1)} %copy.144), channel_id=1, source_target_pairs={{2,0},{4,2},{6,4},{8,6},{10,8},{12,10},{14,12},{16,14},{18,16},{20... | collective-permute-start | bytes 786440 | tf_op jit(solution)/shard_map/ppermute | solution.py:17
  68.8 11.5 %collective-permute-start.4 = (bf16[64,8,256]{2,0,1:T(8,128)(2,1)S(1)}, bf16[64,8,256]{2,0,1:T(8,128)(2,1)S(1)}, u32[]{:S(2)}, u32[]{:S(2)}) collective-permute-start(bf16[64,8,256]{2,0,1:T(8,128)(2,1)S(1)} %get-tuple-element.26), channel_id=1, source_target_pairs={{0,2},{2,4},{4,6},{6,8},{8,10},{10,12},{12,14},{14,16},{16,18},{18... | collective-permute-start | bytes 786440 | tf_op jit(solution)/shard_map/ppermute | solution.py:16
  71.8 8.5 %collective-permute-start.5 = (bf16[64,8,256]{2,0,1:T(8,128)(2,1)S(1)}, bf16[64,8,256]{2,0,1:T(8,128)(2,1)S(1)}, u32[]{:S(2)}, u32[]{:S(2)}) collective-permute-start(bf16[64,8,256]{2,0,1:T(8,128)(2,1)S(1)} %get-tuple-element.27), channel_id=1, source_target_pairs={{2,0},{4,2},{6,4},{8,6},{10,8},{12,10},{14,12},{16,14},{18,16},{20... | collective-permute-start | bytes 786440 | tf_op jit(solution)/shard_map/ppermute | solution.py:17
  75.0 15.6 %collective-permute-start.10 = (bf16[64,32,8]{2,0,1:T(8,128)(2,1)S(1)}, bf16[64,32,8]{2,0,1:T(8,128)(2,1)S(1)}, u32[]{:S(2)}, u32[]{:S(2)}) collective-permute-start(bf16[64,32,8]{2,0,1:T(8,128)(2,1)S(1)} %get-tuple-element.20), channel_id=1, source_target_pairs={{0,1},{2,3},{4,5},{6,7},{8,9},{10,11},{12,13},{14,15},{16,17},{18,... | collective-permute-start | bytes 98312 | tf_op jit(solution)/shard_map/ppermute | solution.py:16
  79.0 16.3 %collective-permute-start.11 = (bf16[64,32,8]{2,0,1:T(8,128)(2,1)S(1)}, bf16[64,32,8]{2,0,1:T(8,128)(2,1)S(1)}, u32[]{:S(2)}, u32[]{:S(2)}) collective-permute-start(bf16[64,32,8]{2,0,1:T(8,128)(2,1)S(1)} %get-tuple-element.21), channel_id=1, source_target_pairs={{1,0},{3,2},{5,4},{7,6},{9,8},{11,10},{13,12},{15,14},{17,16},{19,... | collective-permute-start | bytes 98312 | tf_op jit(solution)/shard_map/ppermute | solution.py:17
  81.7 82.2 %collective-permute-start.6 = (bf16[64,32,8]{2,0,1:T(8,128)(2,1)}, bf16[64,32,8]{2,0,1:T(8,128)(2,1)}, u32[]{:S(2)}, u32[]{:S(2)}) collective-permute-start(bf16[64,32,8]{2,0,1:T(8,128)(2,1)} %get-tuple-element.22), channel_id=1, source_target_pairs={{0,1},{2,3},{4,5},{6,7},{8,9},{10,11},{12,13},{14,15},{16,17},{18,... | collective-permute-start | bytes 98312 | tf_op jit(solution)/shard_map/ppermute | solution.py:16
  87.1 76.8 %collective-permute-start.7 = (bf16[64,32,8]{2,0,1:T(8,128)(2,1)}, bf16[64,32,8]{2,0,1:T(8,128)(2,1)}, u32[]{:S(2)}, u32[]{:S(2)}) collective-permute-start(bf16[64,32,8]{2,0,1:T(8,128)(2,1)} %get-tuple-element.23), channel_id=1, source_target_pairs={{1,0},{3,2},{5,4},{7,6},{9,8},{11,10},{13,12},{15,14},{17,16},{19,... | collective-permute-start | bytes 98312 | tf_op jit(solution)/shard_map/ppermute | solution.py:17
  102.8 61.1 %copy-start.3 = (bf16[64,8,256]{2,0,1:T(8,128)(2,1)S(1)}, bf16[64,8,256]{2,0,1:T(8,128)(2,1)}, u32[]{:S(2)}) copy-start(bf16[64,8,256]{2,0,1:T(8,128)(2,1)} %copy-done.2) | copy-start | bytes 786436
  102.8 236.8 %all-reduce.6.cloned.1.call-start = ((), (), s32[]{:S(2)}) async-start(), calls=%async_computation.1 | async-start | bytes 2031616 | tf_op jit(solution)/shard_map/psum | solution.py:239
  113.1 62.3 %collective-permute-start.12 = (f32[3,8,64]{2,1,0:T(8,128)S(1)}, f32[3,8,64]{2,1,0:T(8,128)S(1)}, u32[]{:S(2)}, u32[]{:S(2)}) collective-permute-start(f32[3,8,64]{2,1,0:T(8,128)S(1)} %get-tuple-element.43), channel_id=1, source_target_pairs={{0,2},{2,4},{4,6},{6,8},{8,10},{10,12},{12,14},{14,16},{16,18},{18... | collective-permute-start | bytes 18440 | tf_op jit(solution)/shard_map/ppermute | solution.py:16
  114.6 60.8 %collective-permute-start.13 = (f32[3,8,64]{2,1,0:T(8,128)S(1)}, f32[3,8,64]{2,1,0:T(8,128)S(1)}, u32[]{:S(2)}, u32[]{:S(2)}) collective-permute-start(f32[3,8,64]{2,1,0:T(8,128)S(1)} %get-tuple-element.44), channel_id=1, source_target_pairs={{2,0},{4,2},{6,4},{8,6},{10,8},{12,10},{14,12},{16,14},{18,16},{20... | collective-permute-start | bytes 18440 | tf_op jit(solution)/shard_map/ppermute | solution.py:17
  173.5 22.9 %copy-start.8 = (bf16[2,3,3,64,64]{4,3,2,1,0:T(8,128)(2,1)S(1)}, bf16[2,3,3,64,64]{4,3,2,1,0:T(8,128)(2,1)}, u32[]{:S(2)}) copy-start(bf16[2,3,3,64,64]{4,3,2,1,0:T(8,128)(2,1)} %param.13) | copy-start | bytes 442372
  197.7 10.6 %copy-start.10 = (bf16[16,256]{1,0:T(8,128)(2,1)S(1)}, bf16[16,256]{1,0:T(8,128)(2,1)}, u32[]{:S(2)}) copy-start(bf16[16,256]{1,0:T(8,128)(2,1)} %param.10) | copy-start | bytes 24580
  197.8 6.0 %collective-permute-start.14 = (f32[3,8,64]{1,2,0:T(8,128)S(1)}, f32[3,8,64]{1,2,0:T(8,128)S(1)}, u32[]{:S(2)}, u32[]{:S(2)}) collective-permute-start(f32[3,8,64]{1,2,0:T(8,128)S(1)} %get-tuple-element.31), channel_id=1, source_target_pairs={{0,1},{2,3},{4,5},{6,7},{8,9},{10,11},{12,13},{14,15},{16,17},{18,... | collective-permute-start | bytes 18440 | tf_op jit(solution)/shard_map/ppermute | solution.py:16
  201.3 6.6 %collective-permute-start.15 = (f32[3,8,64]{1,2,0:T(8,128)S(1)}, f32[3,8,64]{1,2,0:T(8,128)S(1)}, u32[]{:S(2)}, u32[]{:S(2)}) collective-permute-start(f32[3,8,64]{1,2,0:T(8,128)S(1)} %get-tuple-element.32), channel_id=1, source_target_pairs={{1,0},{3,2},{5,4},{7,6},{9,8},{11,10},{13,12},{15,14},{17,16},{19,... | collective-permute-start | bytes 18440 | tf_op jit(solution)/shard_map/ppermute | solution.py:17
  (8 other events, 24.2 us)
Sparse Core Ops, SparseCore 0:
  102.9 92.3 all-reduce.3
  209.1 130.4 all-reduce.5
where the time goes:
time: 353 us; the launch traced here: 352 us
  waiting for transfers between devices  159 us (45%)
  blocking collectives  84.6 us (24%)
  starting transfers between devices  36.4 us (10%)
  matrix products  25.6 us (7%)
  between operations  24.7 us (7%)
  local copies, waits for them, and re-layouts  15.2 us (4%)
  other arithmetic  6.69 us (2%)
    psum x1, waiting for transfers between devices, shards(): lax.psum((grad_row_proj, grad_col_proj, jnp.stack([grad_row_pair, grad_co...  129 us
    psum x1, blocking collectives, shards(): lax.psum((grad_row_proj, grad_col_proj, jnp.stack([grad_row_pair, grad_co...  47.7 us
    ppermute x8, starting transfers between devices, padded_2(): before = lax.ppermute(last, axis, up)  25.9 us
    all_gather x1, blocking collectives, shards(): lax.all_gather(project(col_features, col_proj), 'row', axis=0, tiled=True)  23.3 us
    psum x1, waiting for transfers between devices, shards(): col_sums = lax.psum(col_part, 'row')  19 us
    ppermute x8, starting transfers between devices, padded_2(): after = lax.ppermute(leading, axis, down)  10.5 us
    unnamed x41, local copies, waits for them, and re-layouts  10.3 us
    ppermute x8, waiting for transfers between devices, padded_2(): after = lax.ppermute(leading, axis, down)  8.83 us
  transfers between devices with their start and end apart: 18, of which 5 were waited for; matrix products, arithmetic and copies ran while one was open for 10% of the time, Pallas kernels for 0%

commit v1 on v0

v1 whole, which is shorter than its diff:
```python
import functools

import jax
import jax.numpy as jnp
from jax import lax
from jax.experimental import pallas as pl
from jax.experimental.pallas import tpu as pltpu
from jax.sharding import PartitionSpec as P

MAX_DILATION = 8
LANES = 128
ROW_LANES = 128
F32 = jnp.float32
BF16 = jnp.bfloat16
ALL = ("row", "col")
NT = (((1,), (1,)), ((), ()))
TN = (((0,), (0,)), ((), ()))
GRAD_ROWS = 864


def round_up(value, step):
    return (value + step - 1) // step * step


def mm(a, b):
    return jnp.dot(a, b, preferred_element_type=F32)


def mm_nt(a, b):
    return lax.dot_general(a, b, NT, preferred_element_type=F32)


def mm_tn(a, b):
    return lax.dot_general(a, b, TN, preferred_element_type=F32)


def split(value):
    high = value.astype(BF16)
    low = (value - high.astype(F32)).astype(BF16)
    return high, low


def call(kernel, outs, *args, scratch=(), flops=0, smem=(), mib=20):
    size = sum(a.size * a.dtype.itemsize for a in args)
    size += sum(o.size * o.dtype.itemsize for o in outs)
    specs = [
        pl.BlockSpec(memory_space=pltpu.SMEM if n in smem else pltpu.VMEM)
        for n in range(len(args))
    ]
    return pl.pallas_call(
        kernel,
        out_shape=tuple(outs),
        in_specs=specs,
        out_specs=tuple(pl.BlockSpec(memory_space=pltpu.VMEM) for _ in outs),
        scratch_shapes=list(scratch),
        compiler_params=pltpu.CompilerParams(vmem_limit_bytes=mib << 20),
        cost_estimate=pl.CostEstimate(flops=flops, bytes_accessed=size, transcendentals=0),
    )(*args)


def project_kernel(rf_ref, cf_ref, rp_ref, cp_ref, send_ref):
    devices, chunk, _ = send_ref.shape
    rows = mm(rf_ref[...], rp_ref[...])
    cols = mm(cf_ref[...], cp_ref[...])
    rows = jnp.concatenate([rows, jnp.zeros((chunk - rows.shape[0], 64), F32)], axis=0)
    if cols.shape[0] < chunk:
        cols = jnp.concatenate([cols, jnp.zeros((chunk - cols.shape[0], 64), F32)], axis=0)
    block = jnp.concatenate([cols, rows], axis=1).astype(BF16)

    def put(t, _):
        send_ref[t] = block
        return 0

    lax.fori_loop(0, devices, put, 0)


def back_kernel(dil_ref, cot_ref, weight_ref, rf_ref, cf_ref, dh_ref, shift_ref, feat_ref):
    rate = dil_ref[1]
    rows_here, channels, cols_here = cot_ref.shape
    wide = dh_ref.shape[2]
    margin = MAX_DILATION

    def clear(e, _):
        dh_ref[e] = jnp.zeros((channels, wide), F32)
        return 0

    lax.fori_loop(0, dh_ref.shape[0], clear, 0)
    weight = weight_ref[...]

    def one_row(i, _):
        own = cot_ref[i].astype(F32)
        own = jnp.concatenate([own, jnp.zeros((channels, wide - cols_here), F32)], axis=1)
        left = pltpu.roll(own, wide - rate, 1)
        right = pltpu.roll(own, rate, 1)
        taps = jnp.concatenate([left, own, right], axis=0).astype(BF16)
        shift_ref[i] = taps
        result = mm(weight, taps)
        dh_ref[margin + i - rate] += result[:channels]
        dh_ref[margin + i] += result[channels : 2 * channels] + own
        dh_ref[margin + i + rate] += result[2 * channels :]
        return 0

    lax.fori_loop(0, rows_here, one_row, 0)
    devices, chunk, _ = feat_ref.shape
    rf = rf_ref[...].astype(F32)
    cf = cf_ref[...].astype(F32)
    parts = [rf[:, :LANES], rf[:, LANES:], cf[:, :LANES], cf[:, LANES:]]
    used = sum(p.shape[0] for p in parts)
    if used < chunk:
        parts.append(jnp.zeros((chunk - used, LANES), F32))
    block = jnp.concatenate(parts, axis=0).astype(BF16)

    def put(t, _):
        feat_ref[t] = block
        return 0

    lax.fori_loop(0, devices, put, 0)


def line_taps(line, rate, wide):
    return jnp.concatenate(
        [pltpu.roll(line, rate, 1), line, pltpu.roll(line, wide - rate, 1)], axis=0
    )


def line_back(weight, sums, taps, rate, wide):
    high, low = split(sums)
    back = mm(weight, high) + mm(weight, low)
    n = back.shape[0] // 3
    line = pltpu.roll(back[:n], wide - rate, 1) + back[n : 2 * n]
    line = line + pltpu.roll(back[2 * n :], rate, 1)
    return line, mm_nt(taps, high) + mm_nt(taps, low)


def main_kernel(
    nr, nc, rp, cp, limits,
    dil_ref, recv_ref, wr_ref, wc_ref, bias_ref, dh_ref, shift_ref,
    hidden_ref, send_ref,
    bp_ref, ap_ref, rt_ref, rs_ref, cs_ref, grad_ref, dr_ref, dc_ref, pack_ref,
):
    d1 = dil_ref[0]
    d2 = dil_ref[1]
    r = lax.axis_index("row")
    c = lax.axis_index("col")
    rows_here, cols_here = limits
    ext, channels, wide = dh_ref.shape
    margin = MAX_DILATION
    halo = 2 * margin
    devices = nr * nc
    row_limit = rows_here * nr
    col_limit = cols_here * nc

    bp_ref[...] = jnp.zeros_like(bp_ref)
    ap_ref[...] = jnp.zeros_like(ap_ref)
    for n in range((cols_here + 2 * halo) // cp):
        piece = c * (cols_here // cp) - halo // cp + n
        safe = jnp.clip(piece, 0, devices - 1)
        src = lax.rem(safe, nr) * nc + safe // nr
        scale = jnp.where(piece == safe, 1.0, 0.0).astype(F32)
        at = (n * cp - halo) % wide
        bp_ref[at : at + cp, :] = recv_ref[src].astype(F32)[:cp] * scale
    for n in range((rows_here + 2 * halo) // rp):
        piece = r * (rows_here // rp) - halo // rp + n
        safe = jnp.clip(piece, 0, devices - 1)
        scale = jnp.where(piece == safe, 1.0, 0.0).astype(F32)
        at = (n * rp - halo) % ROW_LANES
        ap_ref[at : at + rp, :] = recv_ref[safe].astype(F32)[:rp] * scale
    b_line = bp_ref[...].T[:channels]
    a_line = ap_ref[...].T[channels:]
    b_taps = line_taps(b_line, d1, wide).astype(BF16)
    a_taps = line_taps(a_line, d1, ROW_LANES).astype(BF16)
    col_terms = mm_tn(wc_ref[...], b_taps)
    row_terms = mm_tn(wr_ref[...], a_taps)
    bias = jnp.broadcast_to(bias_ref[...], (8, LANES)).T[:channels, :1]
    row_terms = jnp.concatenate(
        [
            row_terms[:channels],
            row_terms[channels : 2 * channels] + bias,
            row_terms[2 * channels :],
        ],
        axis=0,
    )
    groups = ext // 8
    for g in range(groups):
        rt_ref[g] = pltpu.roll(row_terms, (margin - 8 * g) % ROW_LANES, 1)

    lane = lax.broadcasted_iota(jnp.int32, (8, wide), 1)[:1]
    place = jnp.where(lane < cols_here + (wide - cols_here) // 2, lane, lane - wide)
    cell = c * cols_here + place
    near = (place >= -margin) & (place < cols_here + margin)
    col_in = jnp.where(near & (cell >= 0) & (cell < col_limit), 1.0, 0.0).astype(F32)
    cv0 = jnp.where(cell - d1 >= 0, 1.0, 0.0).astype(F32)
    cv2 = jnp.where(cell + d1 < col_limit, 1.0, 0.0).astype(F32)
    cs_ref[...] = jnp.zeros_like(cs_ref)
    mark = lax.broadcasted_iota(jnp.int32, (channels, ROW_LANES), 1)
    ct = [col_terms[k * channels : (k + 1) * channels] for k in range(3)]

    def group(g, _):
        terms = rt_ref[g]
        acc = [jnp.zeros((channels, ROW_LANES), F32) for _ in range(3)]
        for u in range(8):
            e = g * 8 + u
            cell_row = r * rows_here + e - margin
            inside = jnp.where((cell_row >= 0) & (cell_row < row_limit), 1.0, 0.0).astype(F32)
            rv0 = jnp.where(cell_row - d1 >= 0, 1.0, 0.0).astype(F32)
            rv2 = jnp.where(cell_row + d1 < row_limit, 1.0, 0.0).astype(F32)
            rt = [terms[k * channels : (k + 1) * channels, u : u + 1] for k in range(3)]
            total = [None, None, None]
            hid = []
            for t in range(wide // LANES):
                s = slice(t * LANES, (t + 1) * LANES)
                pre = ct[1][:, s] + rv0 * ct[0][:, s] + rv2 * ct[2][:, s]
                pre = pre + rt[1] + cv0[:, s] * rt[0] + cv2[:, s] * rt[2]
                sig = 0.5 + 0.5 * jnp.tanh(0.5 * pre)
                mask = col_in[:, s] * inside
                hid.append(((pre * sig) * mask).astype(BF16))
                d = dh_ref[e, :, s] * (sig * (1.0 + pre * (1.0 - sig)) * mask)
                cs_ref[0:channels, s] += rv0 * d
                cs_ref[channels : 2 * channels, s] += d
                cs_ref[2 * channels : 3 * channels, s] += rv2 * d
                part = [d * cv0[:, s], d, d * cv2[:, s]]
                total = [p if o is None else o + p for o, p in zip(total, part)]
            hidden_ref[e] = jnp.concatenate(hid, axis=1)
            for q in range(3):
                line = jnp.sum(total[q], axis=1, keepdims=True)
                acc[q] = jnp.where(mark == u, line, acc[q])
        rs_ref[g] = jnp.concatenate(acc, axis=0)
        return 0

    lax.fori_loop(0, groups, group, 0)

    row_sums = pltpu.roll(rs_ref[0], ROW_LANES - margin, 1)
    for g in range(1, groups):
        row_sums = row_sums + pltpu.roll(rs_ref[g], (8 * g - margin) % ROW_LANES, 1)
    col_sums = cs_ref[...]
    bias_grad = jnp.sum(row_sums[channels : 2 * channels], axis=1, keepdims=True)
    row_line, row_grad = line_back(wr_ref[...], row_sums, a_taps, d1, ROW_LANES)
    col_line, col_grad = line_back(wc_ref[...], col_sums, b_taps, d1, wide)

    conv_grad = jnp.zeros((3 * channels, 3 * channels), F32)
    for i in range(rows_here):
        taps = jnp.concatenate(
            [
                hidden_ref[margin + i - d2],
                hidden_ref[margin + i],
                hidden_ref[margin + i + d2],
            ],
            axis=0,
        )
        conv_grad = conv_grad + mm_nt(taps, shift_ref[i])

    side = 3 * channels
    if grad_ref.shape[0] > GRAD_ROWS:
        grad_ref[GRAD_ROWS:, :] = jnp.zeros((grad_ref.shape[0] - GRAD_ROWS, LANES), F32)
    for n, grad in enumerate((row_grad, col_grad, conv_grad)):
        grad_ref[n * side : (n + 1) * side, :] = grad[:, :LANES]
    grad_ref[3 * side : 4 * side, :64] = row_grad[:, LANES:]
    grad_ref[3 * side : 4 * side, 64:] = col_grad[:, LANES:]
    grad_ref[4 * side : 4 * side + side // 2, :64] = conv_grad[: side // 2, LANES:]
    grad_ref[4 * side : 4 * side + side // 2, 64:] = conv_grad[side // 2 :, LANES:]

    def upright(line):
        n = line.shape[1]
        return jnp.concatenate([line, jnp.zeros((LANES - channels, n), F32)], axis=0).T

    dr = upright(row_line)
    dc = upright(col_line)
    dr_ref[...] = jnp.zeros_like(dr_ref)
    dc_ref[...] = jnp.zeros_like(dc_ref)
    base = pl.multiple_of(r * rows_here, 8)
    dr_ref[pl.ds(base, halo), :] = dr[ROW_LANES - halo :]
    dr_ref[pl.ds(base + halo, rows_here + halo), :] = dr[: rows_here + halo]
    base = pl.multiple_of(c * cols_here, 8)
    dc_ref[pl.ds(base, halo), :] = dc[wide - halo :]
    dc_ref[pl.ds(base + halo, cols_here + halo), :] = dc[: cols_here + halo]

    bias_row = jnp.broadcast_to(bias_grad, (channels, LANES)).T[:1]
    per = grad_ref.shape[0] // devices
    chunk = send_ref.shape[1]
    used = per + rp // 2 + cp // 2 + 1
    if used < chunk:
        pack_ref[used:, :] = jnp.zeros((chunk - used, LANES), F32)
    pack_ref[used - 1 : used, :64] = bias_row
    pack_ref[used - 1 : used, 64:] = jnp.zeros_like(bias_row)
    for t in range(devices):
        tr, tc = divmod(t, nc)
        pack_ref[:per, :] = grad_ref[t * per : (t + 1) * per, :]
        at = halo + t * rp
        pack_ref[per : per + rp // 2, :64] = dr_ref[at : at + rp // 2, :64]
        pack_ref[per : per + rp // 2, 64:] = dr_ref[at + rp // 2 : at + rp, :64]
        at = halo + tc * cols_here + tr * cp
        row = per + rp // 2
        pack_ref[row : row + cp // 2, :64] = dc_ref[at : at + cp // 2, :64]
        pack_ref[row : row + cp // 2, 64:] = dc_ref[at + cp // 2 : at + cp, :64]
        send_ref[t] = pack_ref[...].astype(BF16)


def forward_kernel(dil_ref, hidden_ref, weight_ref, out_ref, taps_ref):
    rate = dil_ref[1]
    rows_here, channels, cols_here = out_ref.shape
    wide = hidden_ref.shape[2]
    margin = MAX_DILATION

    def one_tap(e, _):
        own = hidden_ref[e].astype(F32)
        left = pltpu.roll(own, rate, 1)
        right = pltpu.roll(own, wide - rate, 1)
        taps = jnp.concatenate([left, own, right], axis=0)
        taps_ref[e] = taps[:, :cols_here].astype(BF16)
        return 0

    lax.fori_loop(0, hidden_ref.shape[0], one_tap, 0)
    weight = weight_ref[...]

    def one_row(i, _):
        taps = jnp.concatenate(
            [taps_ref[margin + i - rate], taps_ref[margin + i], taps_ref[margin + i + rate]],
            axis=0,
        )
        own = hidden_ref[margin + i].astype(F32)[:, :cols_here]
        out_ref[i] = (mm(weight, taps) + own).astype(BF16)
        return 0

    lax.fori_loop(0, rows_here, one_row, 0)


def sum_kernel(per, rp, cp, recv_ref, rproj_ref, cproj_ref, send_ref, bias_ref, gr_ref, gc_ref):
    devices = recv_ref.shape[0]

    total = recv_ref[0].astype(F32)
    for t in range(1, devices):
        total = total + recv_ref[t].astype(F32)
    block = total.astype(BF16)

    def put(t, _):
        send_ref[t] = block
        return 0

    lax.fori_loop(0, devices, put, 0)
    used = per + rp // 2 + cp // 2 + 1
    bias_ref[...] = total[used - 1 : used, :]
    dr = total[per : per + rp // 2]
    dc = total[per + rp // 2 : used - 1]
    dr = jnp.concatenate([dr[:, :64], dr[:, 64:]], axis=0).astype(BF16)
    dc = jnp.concatenate([dc[:, :64], dc[:, 64:]], axis=0).astype(BF16)
    gr_ref[...] = mm_nt(dr, rproj_ref[...])
    gc_ref[...] = mm_nt(dc, cproj_ref[...])


def final_kernel(
    per, rp, cp, recv_ref, feat_ref,
    grp_ref, gcp_ref, pair_ref, conv_ref,
    grad_ref, dr_ref, dc_ref, fr_ref, fc_ref,
):
    devices = recv_ref.shape[0]
    for t in range(devices):
        block = recv_ref[t].astype(F32)
        last = min((t + 1) * per, grad_ref.shape[0]) - t * per
        if last > 0:
            grad_ref[t * per : t * per + last, :] = block[:last]
        row = per
        dr_ref[t * rp : t * rp + rp // 2, :] = block[row : row + rp // 2, :64]
        dr_ref[t * rp + rp // 2 : (t + 1) * rp, :] = block[row : row + rp // 2, 64:]
        row = per + rp // 2
        dc_ref[t * cp : t * cp + cp // 2, :] = block[row : row + cp // 2, :64]
        dc_ref[t * cp + cp // 2 : (t + 1) * cp, :] = block[row : row + cp // 2, 64:]
        feat = feat_ref[t].astype(F32)
        fr_ref[t * rp : (t + 1) * rp, :LANES] = feat[:rp]
        fr_ref[t * rp : (t + 1) * rp, LANES:] = feat[rp : 2 * rp]
        row = 2 * rp
        fc_ref[t * cp : (t + 1) * cp, :LANES] = feat[row : row + cp]
        fc_ref[t * cp : (t + 1) * cp, LANES:] = feat[row + cp : row + 2 * cp]
    grp_ref[...] = mm_tn(fr_ref[...].astype(BF16), dr_ref[...].astype(BF16))
    gcp_ref[...] = mm_tn(fc_ref[...].astype(BF16), dc_ref[...].astype(BF16))
    n = 64
    side = 3 * n
    for k in range(3):
        for q in range(3):
            lanes = slice(0, 64) if q != 1 else slice(64, 128)
            at = n * k if q < 2 else 3 * side + n * k
            pair_ref[0, k, q] = grad_ref[at : at + n, lanes]
            lanes = slice(0, 64) if k == 0 else slice(64, 128)
            at = side + n * q if k < 2 else 3 * side + n * q
            pair_ref[1, k, q] = grad_ref[at : at + n, lanes]
            if q < 2:
                at = 2 * side + n * k
                lanes = slice(0, 64) if q == 0 else slice(64, 128)
                conv_ref[k, q] = grad_ref[at : at + n, lanes]
            else:
                at = 4 * side
                half = n // 2
                for h in range(2):
                    line = n * k + half * h
                    lanes = slice(0, 64) if line < side // 2 else slice(64, 128)
                    row = at + line % (side // 2)
                    conv_ref[k, q, half * h : half * (h + 1)] = grad_ref[row : row + half, lanes]


def exchange(value):
    return lax.all_to_all(value, ALL, 0, 0, tiled=True)


def shards(nr, nc, row_features, col_features, row_proj, col_proj, pair_weight, pair_bias,
           conv_weight, dilations, cotangent):
    devices = nr * nc
    channels, rows_here, cols_here = cotangent.shape
    rp, width = row_features.shape
    cp = col_features.shape[0]
    margin = MAX_DILATION
    ext = rows_here + 2 * margin
    wide = cols_here + LANES
    side = 3 * channels
    shape = jax.ShapeDtypeStruct

    chunk_a = round_up(max(rp, cp), 16)
    (line_send,) = call(
        project_kernel,
        [shape((devices, chunk_a, LANES), BF16)],
        row_features, col_features, row_proj, col_proj,
    )
    line_recv = exchange(line_send)

    back_weight = jnp.transpose(conv_weight, (0, 2, 1, 3)).reshape(side, side)
    front_weight = jnp.transpose(conv_weight, (3, 0, 1, 2)).reshape(channels, 3 * side)
    row_weight = jnp.transpose(pair_weight[0], (0, 2, 1, 3)).reshape(side, side)
    col_weight = jnp.transpose(pair_weight[1], (1, 2, 0, 3)).reshape(side, side)
    cot_rows = jnp.transpose(cotangent, (1, 0, 2))
    chunk_f = round_up(2 * rp + 2 * cp, 16)
    d_hidden, shifted, feat_send = call(
        back_kernel,
        [
            shape((ext, channels, wide), F32),
            shape((rows_here, side, wide), BF16),
            shape((devices, chunk_f, LANES), BF16),
        ],
        dilations, cot_rows, back_weight, row_features, col_features,
        smem=(0,), flops=2 * rows_here * side * side * wide,
    )
    feat_recv = exchange(feat_send)

    per = -(-GRAD_ROWS // devices)
    chunk_g = round_up(per + rp // 2 + cp // 2 + 1, 8)
    bias_in = jnp.concatenate([pair_bias, jnp.zeros((LANES - channels,), F32)]).reshape(1, LANES)
    hidden, grad_send = call(
        functools.partial(main_kernel, nr, nc, rp, cp, (rows_here, cols_here)),
        [shape((ext, channels, wide), BF16), shape((devices, chunk_g, LANES), BF16)],
        dilations, line_recv, row_weight, col_weight, bias_in, d_hidden, shifted,
        smem=(0,),
        flops=2 * rows_here * side * side * wide,
        scratch=[
            pltpu.VMEM((wide, LANES), F32),
            pltpu.VMEM((ROW_LANES, LANES), F32),
            pltpu.VMEM((ext // 8, side, ROW_LANES), F32),
            pltpu.VMEM((ext // 8, side, ROW_LANES), F32),
            pltpu.VMEM((side, wide), F32),
            pltpu.VMEM((per * devices, LANES), F32),
            pltpu.VMEM((devices * rp + 4 * margin, LANES), F32),
            pltpu.VMEM((devices * cp + 4 * margin, LANES), F32),
            pltpu.VMEM((chunk_g, LANES), F32),
        ],
    )
    grad_recv = exchange(grad_send)

    (out_rows,) = call(
        forward_kernel,
        [shape((rows_here, channels, cols_here), BF16)],
        dilations, hidden, front_weight,
        smem=(0,),
        flops=2 * rows_here * channels * 3 * side * cols_here,
        scratch=[pltpu.VMEM((ext, side, cols_here), BF16)],
    )
    pair_out = jnp.transpose(out_rows, (1, 0, 2))

    full_send, bias_row, grad_row_features, grad_col_features = call(
        functools.partial(sum_kernel, per, rp, cp),
        [
            shape((devices, chunk_g, LANES), BF16),
            shape((1, LANES), F32),
            shape((rp, width), F32),
            shape((cp, width), F32),
        ],
        grad_recv, row_proj, col_proj,
    )
    full_recv = exchange(full_send)
    grad_row_proj, grad_col_proj, grad_pair_weight, grad_conv_weight = call(
        functools.partial(final_kernel, per, rp, cp),
        [
            shape(row_proj.shape, F32),
            shape(col_proj.shape, F32),
            shape(pair_weight.shape, F32),
            shape(conv_weight.shape, F32),
        ],
        full_recv, feat_recv,
        scratch=[
            pltpu.VMEM((GRAD_ROWS, LANES), F32),
            pltpu.VMEM((devices * rp, channels), F32),
            pltpu.VMEM((devices * cp, channels), F32),
            pltpu.VMEM((devices * rp, width), F32),
            pltpu.VMEM((devices * cp, width), F32),
        ],
    )
    return (
        pair_out,
        grad_row_features,
        grad_col_features,
        grad_row_proj,
        grad_col_proj,
        grad_pair_weight,
        bias_row[0, :channels],
        grad_conv_weight,
    )


def solution(mesh):
    nr, nc = mesh.shape["row"], mesh.shape["col"]
    return jax.shard_map(
        functools.partial(shards, nr, nc),
        mesh=mesh,
        in_specs=(
            P(("row", "col"), None),
            P(("col", "row"), None),
            P(),
            P(),
            P(),
            P(),
            P(),
            P(),
            P(None, "row", "col"),
        ),
        out_specs=(
            P(None, "row", "col"),
            P(("row", "col"), None),
            P(("col", "row"), None),
            P(),
            P(),
            P(),
            P(),
            P(),
        ),
        check_vma=False,
    )
```

time: 353 us -> 91.5 us (0.26)
  waiting for transfers between devices: 159 us -> 14.7 us
  blocking collectives: 84.6 us -> 17.3 us
  matrix products: 25.6 us -> 0 us
  Pallas kernels: 0 us -> 25.6 us
  between operations: 24.7 us -> 0.8 us
  starting transfers between devices: 36.4 us -> 13.1 us
  other arithmetic: 6.69 us -> 0 us
  local copies, waits for them, and re-layouts: 15.2 us -> 19.4 us
    psum x2 -> x0, waiting for transfers between devices: 148 us -> none  [the longest x1 129 us: shards(): lax.psum((grad_row_proj, grad_col_proj, jnp.stack([grad_row_pair, grad_co...]
    psum x2 -> x0, blocking collectives: 56.4 us -> none  [the longest x1 47.7 us: shards(): lax.psum((grad_row_proj, grad_col_proj, jnp.stack([grad_row_pair, grad_co...]
    ppermute x16 -> x0, starting transfers between devices: 36.4 us -> none  [the longest x8 25.9 us: padded_2(): before = lax.ppermute(last, axis, up)]
    all_gather x2 -> x0, blocking collectives: 28.2 us -> none  [the longest x1 23.3 us: shards(): lax.all_gather(project(col_features, col_proj), 'row', axis=0, tiled=True)]
    dot_general x43 -> x0, matrix products: 25.6 us -> none  [the longest x9 4.92 us: back_taps(): jnp.einsum('co,oij->cij', weight[tap_row, tap_col], window, preferred_ele...]
    pallas_call x0 -> x6, Pallas kernels: none -> 25.6 us  [call(): pl.pallas_call(kernel, out_shape=tuple(outs), in_specs=specs, out_specs=t...]
    all_to_all x0 -> x1, blocking collectives: none -> 17.3 us  [exchange(): return lax.all_to_all(value, ALL, 0, 0, tiled=True)]
    all_to_all x0 -> x3, waiting for transfers between devices: none -> 14.7 us  [exchange(): return lax.all_to_all(value, ALL, 0, 0, tiled=True)]
  transfers between devices with their start and end apart: 18 -> 3, of which waited for: 5 -> 2; matrix products, arithmetic and copies ran while one was open for 10% -> 8% of each run, Pallas kernels for 0% -> 15%
where the time goes in v1:
time: 91.5 us; the launch traced here: 90.8 us
  Pallas kernels  25.6 us (28%)
  local copies, waits for them, and re-layouts  19.4 us (21%)
  blocking collectives  17.3 us (19%)
  waiting for transfers between devices  14.7 us (16%)
  starting transfers between devices  13.1 us (14%)
    pallas_call x6, Pallas kernels, call(): pl.pallas_call(kernel, out_shape=tuple(outs), in_specs=specs, out_specs=t...  25.6 us
    all_to_all x1, blocking collectives, exchange(): return lax.all_to_all(value, ALL, 0, 0, tiled=True)  17.3 us
    unnamed x38, local copies, waits for them, and re-layouts  15.6 us
    all_to_all x3, waiting for transfers between devices, exchange(): return lax.all_to_all(value, ALL, 0, 0, tiled=True)  14.7 us
    all_to_all x3, starting transfers between devices, exchange(): return lax.all_to_all(value, ALL, 0, 0, tiled=True)  13.1 us
  transfers between devices with their start and end apart: 3, of which 2 were waited for; matrix products, arithmetic and copies ran while one was open for 8% of the time, Pallas kernels for 15%

profile of v1, /device:TPU:0, one launch (start us, length us, event | category | flops | bytes accessed | tf_op | source)
XLA Modules:
  0.0 90.8 jit_solution(6042512818503789896)
XLA Ops:
  0.7 0.9 copy.29.rp_ref.rproj_ref
  1.6 0.9 copy.30.cp_ref.cproj_ref
  3.9 1.0 %shard_map.152 = bf16[32,16,128]{2,1,0:T(8,128)(2,1)} custom-call(bf16[8,256]{1,0:T(8,128)(2,1)S(1)} %copy-done.10, bf16[16,256]{1,0:T(8,128)(2,1)S(1)} %copy-done.8, bf16[256,64]{1,0:T(8,128)(2,1)S(1)} %copy.29.rp_ref.rproj_ref, bf16[256,64]{1,0:T(8,128)(2,1)S(1)} %copy.30.cp_ref.cproj_ref), custom_call_target="tpu_custom_call" | custom-call | bytes 208896 | tf_op jit(solution)/shard_map/pallas_call | solution.py:50
  4.9 7.3 %all-to-all-start = ((bf16[32,16,128]{2,1,0:T(8,128)(2,1)}), bf16[32,16,128]{2,1,0:T(8,128)(2,1)S(1)}, u32[]{:S(2)}, u32[]{:S(2)}) async-start(bf16[32,16,128]{2,1,0:T(8,128)(2,1)} %shard_map.152), calls=%async_computation | async-start | bytes 262144 | tf_op jit(solution)/shard_map/all_to_all | solution.py:400
  12.2 1.0 %slice_bitcast_fusion = (bf16[3,64,3,64]{3,1,0,2:T(8,128)(2,1)S(1)}, bf16[3,64,3,64]{3,1,2,0:T(8,128)(2,1)S(1)}) fusion(bf16[2,3,3,64,64]{4,3,2,1,0:T(8,128)(2,1)} %param.13), kind=kLoop, calls=%fused_computation.1 | loop fusion | bytes 294912 | tf_op jit(solution)/shard_map/transpose | solution.py:426
  13.2 2.0 %copy.42 = bf16[64,16,256]{2,0,1:T(8,128)(2,1)} copy(bf16[64,16,256]{2,1,0:T(8,128)(2,1)} %param.17) | data formatting | bytes 1048576 | tf_op args[8]
  16.6 0.8 reshape.32.wc_ref
  17.4 1.0 %copy-done.4 = bf16[64,16,256]{2,0,1:T(8,128)(2,1)S(1)} copy-done((bf16[64,16,256]{2,0,1:T(8,128)(2,1)S(1)}, bf16[64,16,256]{2,0,1:T(8,128)(2,1)}, u32[]{:S(2)}) %copy-start.4) | copy-done | bytes 524312
  18.4 0.9 copy-done.7
  19.3 5.7 %shard_map.153 = (f32[32,64,384]{2,1,0:T(8,128)S(1)}, bf16[16,192,384]{2,1,0:T(8,128)(2,1)S(1)}, bf16[32,48,128]{2,1,0:T(8,128)(2,1)S(1)}) custom-call(s32[2]{0:T(128)S(1)} %copy-done.12, bf16[16,64,256]{2,1,0:T(8,128)(2,1)S(1)} %bitcast.21, bf16[192,192]{1,0:T(8,128)(2,1)S(1)} %copy-done.7, bf16[8,256]{1,0:T(8,128)(2,1)S(1)} %copy-done.11, ...), custom_call_target="tpu_custom_call" | custom-call | flops 452984832 | bytes 6508552 | tf_op jit(solution)/shard_map/pallas_call | solution.py:50
  25.0 1.4 %copy-done = bf16[16,192,384]{2,1,0:T(8,128)(2,1)} copy-done((bf16[16,192,384]{2,1,0:T(8,128)(2,1)}, bf16[16,192,384]{2,1,0:T(8,128)(2,1)S(1)}, u32[]{:S(2)}) %copy-start) | copy-done | bytes 2359320
  27.2 1.7 %copy-done.1 = bf16[16,192,384]{2,1,0:T(8,128)(2,1)S(1)} copy-done((bf16[16,192,384]{2,1,0:T(8,128)(2,1)S(1)}, bf16[16,192,384]{2,1,0:T(8,128)(2,1)}, u32[]{:S(2)}) %copy-start.1) | copy-done | bytes 2359320
  28.9 0.9 copy-done.6
  29.8 9.6 %shard_map.154 = (bf16[32,64,384]{2,1,0:T(8,128)(2,1)S(1)}, bf16[32,40,128]{2,1,0:T(8,128)(2,1)S(1)}) custom-call(s32[2]{0:T(128)S(1)} %copy-done.12, bf16[32,16,128]{2,1,0:T(8,128)(2,1)S(1)} %all-to-all-done.recv_ref, bf16[192,192]{1,0:T(8,128)(2,1)S(1)} %reshape.31.wr_ref, bf16[192,192]{1,0:T(8,128)(2,1)S(1)} %copy-done.6, ...), custom_call_target="tpu_custom_call" | custom-call | flops 452984832 | bytes 7684616 | tf_op jit(solution)/shard_map/pallas_call | solution.py:50
  39.4 1.2 %copy-done.2 = bf16[32,64,384]{2,1,0:T(8,128)(2,1)} copy-done((bf16[32,64,384]{2,1,0:T(8,128)(2,1)}, bf16[32,64,384]{2,1,0:T(8,128)(2,1)S(1)}, u32[]{:S(2)}) %copy-start.2) | copy-done | bytes 1572888
  40.6 17.3 %all_to_all.20.recv_ref = bf16[32,40,128]{2,1,0:T(8,128)(2,1)S(1)} all-to-all(bf16[32,40,128]{2,1,0:T(8,128)(2,1)S(1)} %get-tuple-element.24), channel_id=1, replica_groups=mesh['row'=16,'col'=2] {'row','col'}, dimensions={0} | all-to-all | bytes 655360 | tf_op jit(solution)/shard_map/all_to_all | solution.py:400
  57.9 2.7 %all-to-all-start.3 = ((bf16[32,48,128]{2,1,0:T(8,128)(2,1)}), bf16[32,48,128]{2,1,0:T(8,128)(2,1)S(1)}, u32[]{:S(2)}, u32[]{:S(2)}) async-start(bf16[32,48,128]{2,1,0:T(8,128)(2,1)} %copy-done.5), calls=%async_computation.3 | async-start | bytes 786432 | tf_op jit(solution)/shard_map/all_to_all | solution.py:400
  60.6 1.0 %shard_map.156 = (bf16[32,40,128]{2,1,0:T(8,128)(2,1)}, f32[1,128]{1,0:T(1,128)S(1)}, f32[8,256]{1,0:T(8,128)}, f32[16,256]{1,0:T(8,128)}) custom-call(bf16[32,40,128]{2,1,0:T(8,128)(2,1)S(1)} %all_to_all.20.recv_ref, bf16[256,64]{1,0:T(8,128)(2,1)S(1)} %copy.29.rp_ref.rproj_ref, bf16[256,64]{1,0:T(8,128)(2,1)S(1)} %copy.30.cp_ref.cproj_ref), custom_call_target="tpu_custom_call" | custom-call | bytes 745984 | tf_op jit(solution)/shard_map/pallas_call | solution.py:50
  61.6 11.7 %all-to-all-done.3.feat_ref = bf16[32,48,128]{2,1,0:T(8,128)(2,1)S(1)} async-done(((bf16[32,48,128]{2,1,0:T(8,128)(2,1)}), bf16[32,48,128]{2,1,0:T(8,128)(2,1)S(1)}, u32[]{:S(2)}, u32[]{:S(2)}) %all-to-all-start.3) | async-done | bytes 393248 | tf_op jit(solution)/shard_map/all_to_all | solution.py:400
  73.3 3.1 %all-to-all-start.2 = ((bf16[32,40,128]{2,1,0:T(8,128)(2,1)}), bf16[32,40,128]{2,1,0:T(8,128)(2,1)S(1)}, u32[]{:S(2)}, u32[]{:S(2)}) async-start(bf16[32,40,128]{2,1,0:T(8,128)(2,1)} %get-tuple-element.27), calls=%async_computation.2 | async-start | bytes 655360 | tf_op jit(solution)/shard_map/all_to_all | solution.py:400
  76.6 7.0 %shard_map.155 = bf16[16,64,256]{2,1,0:T(8,128)(2,1)S(1)} custom-call(s32[2]{0:T(128)S(1)} %copy-done.12, bf16[32,64,384]{2,1,0:T(8,128)(2,1)S(1)} %copy-done.3, bf16[64,576]{1,0:T(8,128)(2,1)S(1)} %copy.35.weight_ref), custom_call_target="tpu_custom_call" | custom-call | flops 301989888 | bytes 2170888 | tf_op jit(solution)/shard_map/pallas_call | solution.py:50
  83.6 1.1 %copy.38 = bf16[64,16,256]{2,1,0:T(8,128)(2,1)} copy(bf16[64,16,256]{2,0,1:T(8,128)(2,1)S(1)} %bitcast.20) | data formatting | bytes 1048576
  85.1 2.9 %all-to-all-done.2.recv_ref = bf16[32,40,128]{2,1,0:T(8,128)(2,1)S(1)} async-done(((bf16[32,40,128]{2,1,0:T(8,128)(2,1)}), bf16[32,40,128]{2,1,0:T(8,128)(2,1)S(1)}, u32[]{:S(2)}, u32[]{:S(2)}) %all-to-all-start.2) | async-done | bytes 327712 | tf_op jit(solution)/shard_map/all_to_all | solution.py:400
  88.1 1.3 %shard_map.157 = (f32[256,64]{1,0:T(8,128)S(1)}, f32[256,64]{1,0:T(8,128)S(1)}, f32[2,3,3,64,64]{4,3,2,1,0:T(8,128)}, f32[3,3,64,64]{3,2,1,0:T(8,128)}) custom-call(bf16[32,40,128]{2,1,0:T(8,128)(2,1)S(1)} %all-to-all-done.2.recv_ref, bf16[32,48,128]{2,1,0:T(8,128)(2,1)S(1)} %all-to-all-done.3.feat_ref), custom_call_target="tpu_custom_call" | custom-call | bytes 1294336 | tf_op jit(solution)/shard_map/pallas_call | solution.py:50
  (37 shorter events, 5.6 us)
Async XLA Ops:
  0.6 16.7 %copy-start.9 = (bf16[16,256]{1,0:T(8,128)(2,1)S(1)}, bf16[16,256]{1,0:T(8,128)(2,1)}, u32[]{:S(2)}) copy-start(bf16[16,256]{1,0:T(8,128)(2,1)} %cf_ref.3) | copy-start | bytes 24580
  0.6 16.7 %copy-start.11 = (bf16[8,256]{1,0:T(8,128)(2,1)S(1)}, bf16[8,256]{1,0:T(8,128)(2,1)}, u32[]{:S(2)}) copy-start(bf16[8,256]{1,0:T(8,128)(2,1)} %rf_ref.3) | copy-start | bytes 12292
  0.7 14.6 %copy-start.13 = (bf16[3,3,64,64]{3,2,1,0:T(8,128)(2,1)S(1)}, bf16[3,3,64,64]{3,2,1,0:T(8,128)(2,1)}, u32[]{:S(2)}) copy-start(bf16[3,3,64,64]{3,2,1,0:T(8,128)(2,1)} %param.15) | copy-start | bytes 221188
  0.7 16.7 %copy-start.12 = (s32[2]{0:T(128)S(1)}, s32[2]{0:T(128)}, u32[]{:S(2)}) copy-start(s32[2]{0:T(128)} %dil_ref.5) | copy-start | bytes 28
  2.5 0.7 copy-start.8
  3.2 0.7 copy-start.10
  4.9 22.4 %all-to-all-start = ((bf16[32,16,128]{2,1,0:T(8,128)(2,1)}), bf16[32,16,128]{2,1,0:T(8,128)(2,1)S(1)}, u32[]{:S(2)}, u32[]{:S(2)}) async-start(bf16[32,16,128]{2,1,0:T(8,128)(2,1)} %shard_map.152), calls=%async_computation | async-start | bytes 262144 | tf_op jit(solution)/shard_map/all_to_all | solution.py:400
  13.2 14.0 %copy-start.15 = (f32[64]{0:T(128)S(1)}, f32[64]{0:T(128)}, u32[]{:S(2)}) copy-start(f32[64]{0:T(128)} %param.14) | copy-start | bytes 772
  17.4 1.0 %copy-start.4 = (bf16[64,16,256]{2,0,1:T(8,128)(2,1)S(1)}, bf16[64,16,256]{2,0,1:T(8,128)(2,1)}, u32[]{:S(2)}) copy-start(bf16[64,16,256]{2,0,1:T(8,128)(2,1)} %copy.42) | copy-start | bytes 1572868
  18.4 0.9 copy-start.7
  25.0 1.4 %copy-start = (bf16[16,192,384]{2,1,0:T(8,128)(2,1)}, bf16[16,192,384]{2,1,0:T(8,128)(2,1)S(1)}, u32[]{:S(2)}) copy-start(bf16[16,192,384]{2,1,0:T(8,128)(2,1)S(1)} %get-tuple-element.22.shift_ref) | copy-start | bytes 7077892
  26.5 0.7 copy-start.5
  27.2 1.7 %copy-start.1 = (bf16[16,192,384]{2,1,0:T(8,128)(2,1)S(1)}, bf16[16,192,384]{2,1,0:T(8,128)(2,1)}, u32[]{:S(2)}) copy-start(bf16[16,192,384]{2,1,0:T(8,128)(2,1)} %copy-done) | copy-start | bytes 7077892
  28.9 0.9 copy-start.6
  39.4 1.2 %copy-start.2 = (bf16[32,64,384]{2,1,0:T(8,128)(2,1)}, bf16[32,64,384]{2,1,0:T(8,128)(2,1)S(1)}, u32[]{:S(2)}) copy-start(bf16[32,64,384]{2,1,0:T(8,128)(2,1)S(1)} %get-tuple-element.23.hidden_ref) | copy-start | bytes 4718596
  40.6 35.8 %copy-start.14 = (bf16[3,3,64,64]{3,2,1,0:T(8,128)(2,1)S(1)}, bf16[3,3,64,64]{3,2,1,0:T(8,128)(2,1)}, u32[]{:S(2)}) copy-start(bf16[3,3,64,64]{3,2,1,0:T(8,128)(2,1)} %param.15) | copy-start | bytes 221188
  40.6 36.0 %copy-start.3 = (bf16[32,64,384]{2,1,0:T(8,128)(2,1)S(1)}, bf16[32,64,384]{2,1,0:T(8,128)(2,1)}, u32[]{:S(2)}) copy-start(bf16[32,64,384]{2,1,0:T(8,128)(2,1)} %copy-done.2) | copy-start | bytes 4718596
  57.9 15.4 %all-to-all-start.3 = ((bf16[32,48,128]{2,1,0:T(8,128)(2,1)}), bf16[32,48,128]{2,1,0:T(8,128)(2,1)S(1)}, u32[]{:S(2)}, u32[]{:S(2)}) async-start(bf16[32,48,128]{2,1,0:T(8,128)(2,1)} %copy-done.5), calls=%async_computation.3 | async-start | bytes 786432 | tf_op jit(solution)/shard_map/all_to_all | solution.py:400
  73.3 14.8 %all-to-all-start.2 = ((bf16[32,40,128]{2,1,0:T(8,128)(2,1)}), bf16[32,40,128]{2,1,0:T(8,128)(2,1)S(1)}, u32[]{:S(2)}, u32[]{:S(2)}) async-start(bf16[32,40,128]{2,1,0:T(8,128)(2,1)} %get-tuple-element.27), calls=%async_computation.2 | async-start | bytes 655360 | tf_op jit(solution)/shard_map/all_to_all | solution.py:400
